TPU v7x, 32 devices: a whole 2x2x4 slice. The times are simulated.
32 devices in a mesh: groups: 2 (over y), ctx: 4 (over z), tp: 4 (over x, core).
Axes of the slice: x: 2, y: 2, z: 4, core: 2. Of those that a mesh axis runs over, the one named last changes fastest.
Arguments:
- queries: bfloat16 [2048, 5120], P(('groups', 'ctx'), 'tp'), parts along dimension 0, may hold values from -16 to 16
- keys: bfloat16 [2048, 1024], P(('groups', 'ctx'), 'tp'), parts along dimension 0, may hold values from -16 to 16
- values: bfloat16 [2048, 1024], P(('groups', 'ctx'), 'tp'), parts along dimension 0, may hold values from -6 to 6
- positions: int32 [2048], P('groups'), parts along dimension 0, may hold values from 0 to 1023, as said below
- out_weight: bfloat16 [5120, 5120], P('tp', 'ctx'), may hold values from -0.59765625 to 0.59765625
Outputs:
- mixed: bfloat16 [2048, 5120], P(('groups', 'ctx'), 'tp'), parts along dimension 0
There are 2 independent parts, one for each index of `groups`. A program takes and returns all parts, laid end to end along the dimension named above; an argument that names none is the same for every part. Nothing has to cross between parts.
Inputs may be any that keep to these rules, and one draw needn't show every extreme that they name: positions is a permutation of all positions made of 8 aligned runs of 128 consecutive positions, each run increasing.
All inputs are finite; a program needn't handle non-finite values.
Results may differ from a plain program's by a relative error of at most 0.0095.
Values may be sent and summed in bfloat16 or wider, within the bound.
No kernel may reach another device: no remote copies, remote signals or barrier semaphores. Data moves between devices by JAX's collectives and lax.ppermute only.
A program may use at most 64 MiB of HBM per device.

v0:
```python
import math
import jax
import jax.numpy as jnp
from jax import lax
from jax.sharding import PartitionSpec as P

QUERY_HEADS = 40
KEY_VALUE_HEADS = 8
HEAD_SIZE = 128


def local(queries, keys, values, positions, out_weight):
    tok = queries.shape[0]
    kv_heads = keys.shape[1] // HEAD_SIZE
    query_group = QUERY_HEADS // KEY_VALUE_HEADS
    scale = HEAD_SIZE ** (-0.5)
    ctx_index = lax.axis_index("ctx")
    query_pos = lax.dynamic_slice_in_dim(positions, ctx_index * tok, tok)
    query_four = queries.reshape(tok, kv_heads, query_group, HEAD_SIZE)

    def attend(carry, key_block, value_block, key_pos):
        top, total, accum = carry
        count = key_block.shape[0]
        key_three = key_block.reshape(count, kv_heads, HEAD_SIZE)
        value_three = value_block.reshape(count, kv_heads, HEAD_SIZE)
        scores = (
            jnp.einsum("tgjd,kgd->gjtk", query_four, key_three, preferred_element_type=jnp.float32)
            * scale
        )
        keep = key_pos[None, :] <= query_pos[:, None]
        scores = jnp.where(keep, scores, -1e30)
        new_top = jnp.maximum(top, jnp.max(scores, axis=-1))
        factor = jnp.exp(top - new_top)
        expo = jnp.where(keep, jnp.exp(scores - new_top[..., None]), 0.0)
        total = total * factor + jnp.sum(expo, axis=-1)
        weights = expo.astype(jnp.bfloat16)
        accum = accum * factor[..., None] + jnp.einsum(
            "gjtk,kgd->gjtd", weights, value_three, preferred_element_type=jnp.float32
        )
        return (new_top, total, accum)

    start_top = jnp.full((kv_heads, query_group, tok), -1e30, jnp.float32)
    start_total = jnp.zeros((kv_heads, query_group, tok), jnp.float32)
    start_accum = jnp.zeros((kv_heads, query_group, tok, HEAD_SIZE), jnp.float32)
    key_piece = lax.all_gather(keys, "ctx", axis=0, tiled=True)
    value_piece = lax.all_gather(values, "ctx", axis=0, tiled=True)
    rows = key_piece.shape[0]
    width = math.gcd(rows, 512)

    def step(index, state):
        offset = index * width
        key_block = lax.dynamic_slice_in_dim(key_piece, offset, width, 0)
        value_block = lax.dynamic_slice_in_dim(value_piece, offset, width, 0)
        key_pos = lax.dynamic_slice_in_dim(positions, offset, width, 0)
        return attend(state, key_block, value_block, key_pos)

    top, total, accum = lax.fori_loop(0, rows // width, step, (start_top, start_total, start_accum))
    attended = (
        (accum / total[..., None])
        .transpose(2, 0, 1, 3)
        .reshape(tok, kv_heads * query_group * HEAD_SIZE)
        .astype(jnp.bfloat16)
    )
    partial_value = jnp.dot(
        attended,
        lax.all_gather(out_weight, "ctx", axis=1, tiled=True),
        preferred_element_type=jnp.float32,
    )
    summed = lax.psum_scatter(
        partial_value.astype(jnp.bfloat16), "tp", scatter_dimension=1, tiled=True
    )
    return summed


def solution(mesh):
    return jax.shard_map(
        local,
        mesh=mesh,
        in_specs=(
            P(("groups", "ctx"), "tp"),
            P(("groups", "ctx"), "tp"),
            P(("groups", "ctx"), "tp"),
            P("groups"),
            P("tp", "ctx"),
        ),
        out_specs=P(("groups", "ctx"), "tp"),
        check_vma=False,
    )
```

profile of v0, /device:TPU:0, one launch (start us, length us, event | category | flops | bytes accessed | tf_op | source)
XLA Modules:
  0.0 296.8 jit_solution(16109879064267613819)
XLA Ops:
  6.5 0.0 copy-start.1
  6.5 0.0 copy-start.2
  6.5 0.0 copy-start.3
  6.5 0.0 all-gather.2.cloned.1.call-start
  6.5 0.7 all-gather.2.cloned.1.call-update
  7.3 0.0 reduce-scatter.2.cloned.1.call-start
  7.3 1.3 copy.11
  8.7 0.3 copy.13
  9.0 0.0 copy-done.1
  9.0 0.1 copy.12
  9.1 0.0 copy-done.2
  9.1 0.1 copy.10
  9.2 0.0 copy-done.3
  9.2 0.1 dynamic_slice.24
  9.3 19.1 %all_gather.10 = bf16[1024,256]{0,1:T(8,128)(2,1)S(1)} all-gather(bf16[256,256]{0,1:T(8,128)(2,1)S(1)} %copy.12), channel_id=1, replica_groups=mesh['groups'=2,'ctx'=4,'tp'=4] {'ctx'}, dimensions={0}, use_global_device_ids=true | all-gather | bytes 655360 | tf_op jit(solution)/shard_map/all_gather | solution.py:46
  28.4 30.9 %all_gather.9 = bf16[1024,256]{0,1:T(8,128)(2,1)S(1)} all-gather(bf16[256,256]{0,1:T(8,128)(2,1)S(1)} %copy.10), channel_id=1, replica_groups=mesh['groups'=2,'ctx'=4,'tp'=4] {'ctx'}, dimensions={0}, use_global_device_ids=true | all-gather | bytes 655360 | tf_op jit(solution)/shard_map/all_gather | solution.py:45
  59.3 19.9 %while.18 = (s32[]{:T(128)}, f32[2,5,256]{2,1,0:T(8,128)S(1)}, f32[2,5,256]{2,1,0:T(8,128)S(1)}, f32[2,5,256,128]{3,2,1,0:T(8,128)S(1)}, s32[1024]{0:T(1024)S(1)...) while((s32[]{:T(128)}, f32[2,5,256]{2,1,0:T(8,128)S(1)}, ...), condition=%wide.region_3.4_spmd.clone, body=%wide.region_0.3_spmd.clone.sunk | while | flops 689254912 | bytes 42245336 | solution.py:57
  59.3 0.1 dynamic_slice.33
  59.3 0.1 broadcast_compare_fusion.2
  59.6 3.3 %fusion.30 = (f32[2,5,256]{2,1,0:T(8,128)S(1)}, f32[2,512,256,5]{2,1,3,0:T(8,128)}) fusion(pred[256,512]{0,1:T(8,128)(4,1)S(1)} %broadcast_compare_fusion.2, bf16[512,2,128,1]{0,2,3,1:T(8,128)(2,1)S(1)} %bitcast.48, bf16[256,2,5,128]{3,0,2,1:T(8,128)(2,1)S(1)} %get-tuple-element.325), kind=kOutput, calls=%fused_computation.2.clone.1 | convolution fusion | flops 339473920 | bytes 6301696 | tf_op jit(solution)/shard_map/while/body/eval_jaxpr/tgjd,kgd->gjtk/dot_general | solution.py:27
  62.9 0.0 copy-start
  62.9 4.0 %fusion.31 = f32[2,5,256]{2,1,0:T(8,128)S(1)} fusion(f32[2,512,256,5]{2,1,3,0:T(8,128)} %get-tuple-element.288, f32[2,5,256]{2,1,0:T(8,128)S(1)} %select_maximum_fusion.2, pred[256,512]{0,1:T(8,128)(4,1)S(1)} %broadcast_compare_fusion.2), kind=kLoop, calls=%fused_computation.4.clone.1 | loop fusion | flops 6551040 | bytes 5394432 | tf_op jit(solution)/shard_map/while/body/eval_jaxpr/reduce_sum | solution.py:35
  66.9 0.2 copy-done
  67.1 2.2 fusion.33
  69.3 0.1 dynamic_slice.33
  69.4 0.1 broadcast_compare_fusion.2
  69.6 3.3 %fusion.30 = (f32[2,5,256]{2,1,0:T(8,128)S(1)}, f32[2,512,256,5]{2,1,3,0:T(8,128)}) fusion(pred[256,512]{0,1:T(8,128)(4,1)S(1)} %broadcast_compare_fusion.2, bf16[512,2,128,1]{0,2,3,1:T(8,128)(2,1)S(1)} %bitcast.48, bf16[256,2,5,128]{3,0,2,1:T(8,128)(2,1)S(1)} %get-tuple-element.325), kind=kOutput, calls=%fused_computation.2.clone.1 | convolution fusion | flops 339473920 | bytes 6301696 | tf_op jit(solution)/shard_map/while/body/eval_jaxpr/tgjd,kgd->gjtk/dot_general | solution.py:27
  72.9 0.0 copy-start
  72.9 3.9 %fusion.31 = f32[2,5,256]{2,1,0:T(8,128)S(1)} fusion(f32[2,512,256,5]{2,1,3,0:T(8,128)} %get-tuple-element.288, f32[2,5,256]{2,1,0:T(8,128)S(1)} %select_maximum_fusion.2, pred[256,512]{0,1:T(8,128)(4,1)S(1)} %broadcast_compare_fusion.2), kind=kLoop, calls=%fused_computation.4.clone.1 | loop fusion | flops 6551040 | bytes 5394432 | tf_op jit(solution)/shard_map/while/body/eval_jaxpr/reduce_sum | solution.py:35
  76.8 0.1 copy-done
  77.0 2.2 fusion.33
  79.2 0.4 copy.14
  79.6 0.1 divide_convert_fusion
  79.8 167.2 %all-gather.2.cloned.1.call-done = bf16[1280,5120]{1,0:T(8,128)(2,1)} async-done(((bf16[1280,1280]{1,0:T(8,128)(2,1)}), bf16[1280,5120]{1,0:T(8,128)(2,1)}) %all-gather.2.cloned.1.call-update) | async-done | bytes 13107216 | tf_op jit(solution)/shard_map/all_gather | solution.py:66
  247.0 9.7 %convolution_convert_fusion = bf16[256,5120]{1,0:T(8,128)(2,1)} fusion(bf16[256,1280]{0,1:T(8,128)(2,1)S(1)} %bitcast.50, bf16[1280,5120]{1,0:T(8,128)(2,1)} %all-gather.2.cloned.1.call-done), kind=kOutput, calls=%fused_computation.19 | convolution fusion | flops 3356753920 | bytes 16384000 | tf_op jit(solution)/shard_map/dot_general | solution.py:64
  256.7 0.0 reduce-scatter.2.cloned.1.call-update
  256.7 33.3 %reduce-scatter.2.cloned.1.call-done = bf16[256,1280]{1,0:T(8,128)(2,1)} async-done(((bf16[256,5120]{1,0:T(8,128)(2,1)}), bf16[256,1280]{1,0:T(8,128)(2,1)}) %reduce-scatter.2.cloned.1.call-update) | async-done | bytes 655376 | tf_op jit(solution)/shard_map/reduce_scatter | solution.py:69
  (11 shorter events, 0.1 us)
Async XLA Ops:
  6.5 2.5 copy-start.1
  6.5 2.6 copy-start.2
  6.5 2.7 copy-start.3
  6.5 240.4 %all-gather.2.cloned.1.call-start = ((), (), s32[]{:S(2)}) async-start(), calls=%async_computation.1 | async-start | bytes 16384000 | tf_op jit(solution)/shard_map/all_gather | solution.py:66
  7.3 282.7 %reduce-scatter.2.cloned.1.call-start = ((), (), s32[]{:S(2)}) async-start(), calls=%async_computation.2 | async-start | bytes 3276800 | tf_op jit(solution)/shard_map/reduce_scatter | solution.py:69
  62.9 4.2 %copy-start = (f32[2,512,256,5]{2,1,3,0:T(8,128)S(1)}, f32[2,512,256,5]{2,1,3,0:T(8,128)}, u32[]{:S(2)}) copy-start(f32[2,512,256,5]{2,1,3,0:T(8,128)} %get-tuple-element.288) | copy-start | bytes 15728644 | tf_op jit(solution)/shard_map/while
  72.9 4.0 %copy-start = (f32[2,512,256,5]{2,1,3,0:T(8,128)S(1)}, f32[2,512,256,5]{2,1,3,0:T(8,128)}, u32[]{:S(2)}) copy-start(f32[2,512,256,5]{2,1,3,0:T(8,128)} %get-tuple-element.288) | copy-start | bytes 15728644 | tf_op jit(solution)/shard_map/while
Sparse Core Ops, SparseCore 0:
  8.9 238.0 all-gather.1
  256.8 33.1 reduce-scatter.1
where the time goes:
time: 297 us
  waiting for transfers between devices  201 us (68%)
  blocking collectives  49.9 us (17%)
  matrix products  20.8 us (7%)
  between operations  13.5 us (5%)
  other arithmetic  8.32 us (3%)
    all_gather x1, waiting for transfers between devices, local(): lax.all_gather(out_weight, 'ctx', axis=1, tiled=True)  167 us
    reduce_scatter x1, waiting for transfers between devices, local(): lax.psum_scatter(partial_value.astype(jnp.bfloat16), 'tp', scatter_dimens...  33.3 us
    all_gather x1, blocking collectives, local(): key_piece = lax.all_gather(keys, 'ctx', axis=0, tiled=True)  30.9 us
    all_gather x1, blocking collectives, local(): value_piece = lax.all_gather(values, 'ctx', axis=0, tiled=True)  19.1 us
    dot_general x1, matrix products, local(): jnp.dot(attended, lax.all_gather(out_weight, 'ctx', axis=1, tiled=True),...  9.69 us
    reduce_sum x2, other arithmetic, attend(): total = total * factor + jnp.sum(expo, axis=-1)  7.85 us
    dot_general x2, matrix products, attend(): jnp.einsum('tgjd,kgd->gjtk', query_four, key_three, preferred_element_typ...  6.64 us
  transfers between devices with their start and end apart: 2, of which 2 were waited for; matrix products, arithmetic and copies ran while one was open for 7% of the time, Pallas kernels for 0%

commit v1 on v0

--- a/solution.py
+++ b/solution.py
@@ -42,8 +42,11 @@
     start_top = jnp.full((kv_heads, query_group, tok), -1e30, jnp.float32)
     start_total = jnp.zeros((kv_heads, query_group, tok), jnp.float32)
     start_accum = jnp.zeros((kv_heads, query_group, tok, HEAD_SIZE), jnp.float32)
-    key_piece = lax.all_gather(keys, "ctx", axis=0, tiled=True)
-    value_piece = lax.all_gather(values, "ctx", axis=0, tiled=True)
+    key_piece, value_piece = jnp.split(
+        lax.all_gather(jnp.concatenate([keys, values], axis=1), "ctx", axis=0, tiled=True),
+        [keys.shape[1]],
+        axis=1,
+    )
     rows = key_piece.shape[0]
     width = math.gcd(rows, 512)
 

time: 297 us -> 318 us (1.071)
  waiting for transfers between devices: 201 us -> 267 us
  blocking collectives: 49.9 us -> 0 us
  local copies, waits for them, and re-layouts: 2.89 us -> 6.76 us
    all_gather x2 -> x0, blocking collectives: 49.9 us -> none  [the longest x1 30.9 us: local(): key_piece = lax.all_gather(keys, 'ctx', axis=0, tiled=True)]
    all_gather x1, waiting for transfers between devices: 167 us -> 203 us  [local(): lax.all_gather(out_weight, 'ctx', axis=1, tiled=True)]
    all_gather x0 -> x1, waiting for transfers between devices: none -> 30.2 us  [local(): lax.all_gather(jnp.concatenate([keys, values], axis=1), 'ctx', axis=0, ti...]
  transfers between devices with their start and end apart: 2 -> 3, of which waited for: 2 -> 3; matrix products, arithmetic and copies ran while one was open for 7% -> 7% of each run, Pallas kernels for 0% -> 0%
where the time goes in v1:
time: 318 us
  waiting for transfers between devices  267 us (84%)
  matrix products  20.7 us (7%)
  between operations  13.2 us (4%)
  other arithmetic  9.68 us (3%)
  local copies, waits for them, and re-layouts  6.76 us (2%)
    all_gather x1, waiting for transfers between devices, local(): lax.all_gather(out_weight, 'ctx', axis=1, tiled=True)  203 us
    reduce_scatter x1, waiting for transfers between devices, local(): lax.psum_scatter(partial_value.astype(jnp.bfloat16), 'tp', scatter_dimens...  32.7 us
    all_gather x1, waiting for transfers between devices, local(): lax.all_gather(jnp.concatenate([keys, values], axis=1), 'ctx', axis=0, ti...  30.2 us
    dot_general x1, matrix products, local(): jnp.dot(attended, lax.all_gather(out_weight, 'ctx', axis=1, tiled=True),...  9.67 us
    reduce_sum x2, other arithmetic, attend(): total = total * factor + jnp.sum(expo, axis=-1)  8.5 us
    dot_general x2, matrix products, attend(): jnp.einsum('tgjd,kgd->gjtk', query_four, key_three, preferred_element_typ...  6.62 us
  transfers between devices with their start and end apart: 3, of which 3 were waited for; matrix products, arithmetic and copies ran while one was open for 7% of the time, Pallas kernels for 0%

profile of v1, /device:TPU:0, one launch (start us, length us, event | category | flops | bytes accessed | tf_op | source)
XLA Modules:
  0.0 317.7 jit_solution(3241197346551124525)
XLA Ops:
  6.5 0.0 copy-start.1
  6.5 0.0 all-gather.3.cloned.1.call-start
  6.5 1.0 copy.10
  7.6 1.0 copy.11
  8.6 0.7 pad_maximum_fusion
  9.3 0.0 all-gather.3.cloned.1.call-update
  9.3 0.0 all-gather.5.cloned.1.call-start
  9.4 0.7 all-gather.5.cloned.1.call-update
  10.1 0.0 reduce-scatter.2.cloned.1.call-start
  10.2 1.3 copy.12
  11.5 0.3 copy.13
  11.8 0.0 copy-done.1
  11.8 0.1 dynamic_slice.24
  11.9 30.2 %all-gather.3.cloned.1.call-done = bf16[1024,512]{0,1:T(8,128)(2,1)} async-done(((bf16[256,512]{0,1:T(8,128)(2,1)}), bf16[1024,512]{0,1:T(8,128)(2,1)}) %all-gather.3.cloned.1.call-update) | async-done | bytes 1048592 | tf_op jit(solution)/shard_map/all_gather | solution.py:46
  42.1 1.3 fusion.13
  43.4 21.4 %while.18 = (s32[]{:T(128)}, f32[2,5,256]{2,1,0:T(8,128)S(1)}, f32[2,5,256]{2,1,0:T(8,128)S(1)}, f32[2,5,256,128]{3,2,1,0:T(8,128)S(1)}, s32[1024]{0:T(1024)S(1)...) while((s32[]{:T(128)}, f32[2,5,256]{2,1,0:T(8,128)S(1)}, ...), condition=%wide.region_3.4_spmd.clone, body=%wide.region_0.3_spmd.clone.sunk | while | flops 689254912 | bytes 42245336 | solution.py:60
  43.4 0.1 dynamic_slice.33
  43.5 0.1 broadcast_compare_fusion.2
  43.7 3.3 %fusion.31 = (f32[2,5,256]{2,1,0:T(8,128)S(1)}, f32[2,512,256,5]{2,1,3,0:T(8,128)}) fusion(pred[256,512]{0,1:T(8,128)(4,1)S(1)} %broadcast_compare_fusion.2, bf16[512,2,128,1]{0,2,3,1:T(8,128)(2,1)S(1)} %bitcast.48, bf16[256,2,5,128]{3,0,2,1:T(8,128)(2,1)S(1)} %get-tuple-element.327), kind=kOutput, calls=%fused_computation.2.clone.1 | convolution fusion | flops 339473920 | bytes 6301696 | tf_op jit(solution)/shard_map/while/body/eval_jaxpr/tgjd,kgd->gjtk/dot_general | solution.py:27
  47.0 0.0 copy-start
  47.0 4.5 %fusion.32 = f32[2,5,256]{2,1,0:T(8,128)S(1)} fusion(f32[2,512,256,5]{2,1,3,0:T(8,128)} %get-tuple-element.290, f32[2,5,256]{2,1,0:T(8,128)S(1)} %select_maximum_fusion.2, pred[256,512]{0,1:T(8,128)(4,1)S(1)} %broadcast_compare_fusion.2), kind=kLoop, calls=%fused_computation.4.clone.1 | loop fusion | flops 6551040 | bytes 5394432 | tf_op jit(solution)/shard_map/while/body/eval_jaxpr/reduce_sum | solution.py:35
  51.6 0.9 copy-done
  52.5 2.2 fusion.34
  54.7 0.1 dynamic_slice.33
  54.8 0.1 broadcast_compare_fusion.2
  55.0 3.3 %fusion.31 = (f32[2,5,256]{2,1,0:T(8,128)S(1)}, f32[2,512,256,5]{2,1,3,0:T(8,128)}) fusion(pred[256,512]{0,1:T(8,128)(4,1)S(1)} %broadcast_compare_fusion.2, bf16[512,2,128,1]{0,2,3,1:T(8,128)(2,1)S(1)} %bitcast.48, bf16[256,2,5,128]{3,0,2,1:T(8,128)(2,1)S(1)} %get-tuple-element.327), kind=kOutput, calls=%fused_computation.2.clone.1 | convolution fusion | flops 339473920 | bytes 6301696 | tf_op jit(solution)/shard_map/while/body/eval_jaxpr/tgjd,kgd->gjtk/dot_general | solution.py:27
  58.3 0.0 copy-start
  58.4 4.0 %fusion.32 = f32[2,5,256]{2,1,0:T(8,128)S(1)} fusion(f32[2,512,256,5]{2,1,3,0:T(8,128)} %get-tuple-element.290, f32[2,5,256]{2,1,0:T(8,128)S(1)} %select_maximum_fusion.2, pred[256,512]{0,1:T(8,128)(4,1)S(1)} %broadcast_compare_fusion.2), kind=kLoop, calls=%fused_computation.4.clone.1 | loop fusion | flops 6551040 | bytes 5394432 | tf_op jit(solution)/shard_map/while/body/eval_jaxpr/reduce_sum | solution.py:35
  62.4 0.2 copy-done
  62.5 2.2 fusion.34
  64.8 0.4 copy.14
  65.2 0.1 divide_convert_fusion
  65.3 203.5 %all-gather.5.cloned.1.call-done = bf16[1280,5120]{1,0:T(8,128)(2,1)} async-done(((bf16[1280,1280]{1,0:T(8,128)(2,1)}), bf16[1280,5120]{1,0:T(8,128)(2,1)}) %all-gather.5.cloned.1.call-update) | async-done | bytes 13107216 | tf_op jit(solution)/shard_map/all_gather | solution.py:69
  268.8 9.7 %convolution_convert_fusion = bf16[256,5120]{1,0:T(8,128)(2,1)} fusion(bf16[256,1280]{0,1:T(8,128)(2,1)S(1)} %bitcast.50, bf16[1280,5120]{1,0:T(8,128)(2,1)} %all-gather.5.cloned.1.call-done), kind=kOutput, calls=%fused_computation.19 | convolution fusion | flops 3356753920 | bytes 16384000 | tf_op jit(solution)/shard_map/dot_general | solution.py:67
  278.4 0.0 reduce-scatter.2.cloned.1.call-update
  278.5 32.7 %reduce-scatter.2.cloned.1.call-done = bf16[256,1280]{1,0:T(8,128)(2,1)} async-done(((bf16[256,5120]{1,0:T(8,128)(2,1)}), bf16[256,1280]{1,0:T(8,128)(2,1)}) %reduce-scatter.2.cloned.1.call-update) | async-done | bytes 655376 | tf_op jit(solution)/shard_map/reduce_scatter | solution.py:72
  (11 shorter events, 0.1 us)
Async XLA Ops:
  6.5 5.3 %copy-start.1 = (s32[1024]{0:T(1024)S(1)}, s32[1024]{0:T(1024)}, u32[]{:S(2)}) copy-start(s32[1024]{0:T(1024)} %param.10) | copy-start | bytes 12292
  6.5 35.6 %all-gather.3.cloned.1.call-start = ((), (), s32[]{:S(2)}) async-start(), calls=%async_computation.1 | async-start | bytes 1310720 | tf_op jit(solution)/shard_map/all_gather | solution.py:46
  9.3 259.5 %all-gather.5.cloned.1.call-start = ((), (), s32[]{:S(2)}) async-start(), calls=%async_computation.2 | async-start | bytes 16384000 | tf_op jit(solution)/shard_map/all_gather | solution.py:69
  10.1 301.1 %reduce-scatter.2.cloned.1.call-start = ((), (), s32[]{:S(2)}) async-start(), calls=%async_computation.3 | async-start | bytes 3276800 | tf_op jit(solution)/shard_map/reduce_scatter | solution.py:72
  47.0 5.5 %copy-start = (f32[2,512,256,5]{2,1,3,0:T(8,128)S(1)}, f32[2,512,256,5]{2,1,3,0:T(8,128)}, u32[]{:S(2)}) copy-start(f32[2,512,256,5]{2,1,3,0:T(8,128)} %get-tuple-element.290) | copy-start | bytes 15728644 | tf_op jit(solution)/shard_map/while
  58.3 4.2 %copy-start = (f32[2,512,256,5]{2,1,3,0:T(8,128)S(1)}, f32[2,512,256,5]{2,1,3,0:T(8,128)}, u32[]{:S(2)}) copy-start(f32[2,512,256,5]{2,1,3,0:T(8,128)} %get-tuple-element.290) | copy-start | bytes 15728644 | tf_op jit(solution)/shard_map/while
Sparse Core Ops, SparseCore 0:
  9.4 32.6 all-gather.2
  43.7 225.0 all-gather.4
  278.6 32.5 reduce-scatter.1
